TPU v7x, 32 devices: a whole 2x2x4 slice. The times are simulated.
32 devices in a mesh: dp: 4 (over y, core), tp: 8 (over z, x).
Axes of the slice: x: 2, y: 2, z: 4, core: 2. Of those that a mesh axis runs over, the one named last changes fastest.
Arguments:
- teacher_partial: bfloat16 [8, 512, 4608], P('tp', 'dp'), may hold values from -5 to 5
- teacher_residual: bfloat16 [512, 4608], P(('dp', 'tp')), may hold values from -120 to 120
- post_gain: float32 [4608], replicated, may hold values from 0.5 to 1.5
- final_gain: float32 [4608], replicated, may hold values from 0.5 to 1.5
- teacher_head: bfloat16 [4608, 32768], P(None, ('dp', 'tp')), may hold values from -40 to 40
- student_hidden: bfloat16 [512, 3584], P(('dp', 'tp')), may hold values from -120 to 120
- student_gain: float32 [3584], replicated, may hold values from 0.5 to 1.5
- student_head: bfloat16 [3584, 32768], P(None, ('dp', 'tp')), may hold values from -40 to 40
- labels: int32 [512], P('dp'), may hold values from 0 to 32767
- lengths: int32 [4, 8], P('dp'), may hold values from 1 to 48, 96 in all within a row
Outputs:
- grad_hidden: float32 [512, 3584], P(('dp', 'tp'))
- token_loss: float32 [512], P(('dp', 'tp'))
Inputs may be any that keep to these rules, and one draw needn't show every extreme that they name: `lengths`: group g's 8 sequences fill, in order, its first 96 rows; its remaining 128 - 96 rows are padding.
All inputs are finite; a program needn't handle non-finite values.
Results may differ from a plain program's by a relative error of at most 0.03.
Values may be sent and summed in bfloat16 or wider, within the bound.
No kernel may reach another device: no remote copies, remote signals or barrier semaphores. Data moves between devices by JAX's collectives and lax.ppermute only.
A program may use at most 128 MiB of HBM per device.

v0:
```python
import jax
import jax.numpy as jnp
from jax import lax
from jax.sharding import PartitionSpec as P

EPS = 1e-06
BETA = 0.5
LOSS_SCALE = 1024.0


def norm_rows(values, gain):
    inverse = lax.rsqrt(jnp.mean(values * values, axis=-1, keepdims=True) + EPS)
    return (values * inverse * gain, inverse)


def token_weights(lengths, tok_rows):
    ends = jnp.cumsum(lengths, axis=1)
    starts = ends - lengths
    places = jnp.arange(tok_rows, dtype=jnp.int32)
    inside = (places[None, :, None] >= starts[:, None, :]) & (
        places[None, :, None] < ends[:, None, :]
    )
    spans = jnp.sum(jnp.where(inside, lengths[:, None, :], 0), axis=2)
    covered = jnp.sum(inside.astype(jnp.int32), axis=2)
    return covered.astype(jnp.float32) / jnp.maximum(spans, 1).astype(jnp.float32)


def shards(
    teacher_partial,
    teacher_residual,
    post_gain,
    final_gain,
    teacher_head,
    student_hidden,
    student_gain,
    student_head,
    labels,
    lengths,
):
    share = teacher_residual.shape[0]
    tok_rows = labels.shape[0]
    mlp_sum = lax.psum_scatter(
        teacher_partial[0].astype(jnp.float32).astype(jnp.bfloat16),
        "tp",
        scatter_dimension=0,
        tiled=True,
    ).astype(jnp.float32)
    post, unused = norm_rows(mlp_sum, post_gain)
    final = teacher_residual.astype(jnp.float32) + post
    teacher_norm = norm_rows(final, final_gain)[0].astype(jnp.bfloat16)
    student_f = student_hidden.astype(jnp.float32)
    student_scaled, inverse = norm_rows(student_f, student_gain)
    student_norm = student_scaled.astype(jnp.bfloat16)
    label_all, length_all = (
        lax.all_gather(labels, "dp", axis=0, tiled=True),
        lax.all_gather(lengths, "dp", axis=0, tiled=True),
    )
    groups = length_all.shape[0]
    weight_all = token_weights(length_all, tok_rows)
    whole_t, whole_s = (
        lax.all_gather(teacher_norm, ("dp", "tp"), axis=0, tiled=True),
        lax.all_gather(student_norm, ("dp", "tp"), axis=0, tiled=True),
    )
    label_rows = label_all.reshape(groups, tok_rows).reshape(-1)
    weight_rows = weight_all.reshape(-1)
    vocab_dev = teacher_head.shape[1]
    position = lax.axis_index("dp") * lax.axis_size("tp") + lax.axis_index("tp")
    columns = position * vocab_dev + jnp.arange(vocab_dev, dtype=jnp.int32)
    t_logits = jnp.dot(whole_t, teacher_head, preferred_element_type=jnp.float32)
    s_logits = jnp.dot(whole_s, student_head, preferred_element_type=jnp.float32)
    hit = label_rows[:, None] == columns[None, :]
    label_logit = jnp.sum(jnp.where(hit, s_logits, 0.0), axis=1)
    t_local = jnp.max(t_logits, axis=1)
    s_local = jnp.max(s_logits, axis=1)
    t_max, s_max = lax.pmax((t_local, s_local), ("dp", "tp"))
    t_exp = jnp.exp(t_logits - t_max[:, None])
    s_exp = jnp.exp(s_logits - s_max[:, None])
    t_total, t_cross, s_total, label_value = lax.psum(
        (
            jnp.sum(t_exp, axis=1),
            jnp.sum(t_exp * (t_logits - s_logits), axis=1),
            jnp.sum(s_exp, axis=1),
            label_logit,
        ),
        ("dp", "tp"),
    )
    t_log = t_max + jnp.log(t_total)
    s_log = s_max + jnp.log(s_total)
    divergence = t_cross / t_total - t_log + s_log
    label_term = s_log - label_value
    row_loss = jnp.where(weight_rows > 0, divergence + BETA * label_term, 0.0)
    t_prob = t_exp / t_total[:, None]
    s_prob = s_exp / s_total[:, None]
    scale = (LOSS_SCALE * weight_rows)[:, None]
    logit_grad = (scale * ((1.0 + BETA) * s_prob - t_prob - BETA * hit.astype(jnp.float32))).astype(
        jnp.bfloat16
    )
    summed = lax.psum_scatter(
        lax.dot_general(
            logit_grad, student_head, (((1,), (1,)), ((), ())), preferred_element_type=jnp.float32
        ),
        ("dp", "tp"),
        scatter_dimension=0,
        tiled=True,
    )
    scaled = summed * student_gain
    inner = jnp.mean(scaled * student_f, axis=1, keepdims=True)
    grad_hidden = inverse * scaled - student_f * (inverse * inverse * inverse) * inner
    token_loss = lax.dynamic_slice_in_dim(row_loss, position * share, share, 0)
    return (grad_hidden, token_loss)


def solution(mesh):
    placed = (
        P("tp", "dp", None),
        P(("dp", "tp"), None),
        P(),
        P(),
        P(None, ("dp", "tp")),
        P(("dp", "tp"), None),
        P(),
        P(None, ("dp", "tp")),
        P("dp"),
        P("dp", None),
    )
    return jax.shard_map(
        shards,
        mesh=mesh,
        in_specs=placed,
        out_specs=(P(("dp", "tp"), None), P(("dp", "tp"))),
        check_vma=False,
    )
```

profile of v0, /device:TPU:0, one launch (start us, length us, event | category | flops | bytes accessed | tf_op | source)
XLA Modules:
  0.0 426.0 jit_solution(3692011497358117005)
XLA Ops:
  8.1 0.7 reduce-scatter.3.cloned.1.call-update
  8.8 1.0 fusion.21
  9.9 1.7 fusion.23
  11.6 0.0 all-gather.7.cloned.1.call-start
  11.6 70.1 %reduce-scatter.3.cloned.1.call-done = bf16[16,4608]{1,0:T(8,128)(2,1)} async-done(((bf16[128,4608]{1,0:T(8,128)(2,1)}), bf16[16,4608]{1,0:T(8,128)(2,1)}) %reduce-scatter.3.cloned.1.call-update) | async-done | bytes 147472 | tf_op jit(solution)/shard_map/reduce_scatter | solution.py:42
  81.7 1.1 fusion.18
  82.8 1.2 multiply_reduce_fusion.1
  84.0 1.7 multiply_convert_fusion
  85.8 0.0 reduce-scatter.5.cloned.1.call-start
  85.8 5.1 %all-gather = s32[4,1,8]{2,1,0:T(1,128)S(1)} all-gather(s32[1,1,8]{2,1,0:T(1,128)S(1)} %bitcast.20), channel_id=1, replica_groups=mesh['dp'=4,'tp'=8] {'dp'}, dimensions={0}, use_global_device_ids=true | all-gather | bytes 160 | tf_op jit(solution)/shard_map/all_gather | solution.py:56
  90.9 0.2 reduce_window_sum.11
  91.1 5.0 %all-gather.1 = s32[4,1,128]{2,1,0:T(1,128)S(1)} all-gather(s32[1,1,128]{2,1,0:T(1,128)S(1)} %bitcast.21), channel_id=1, replica_groups=mesh['dp'=4,'tp'=8] {'dp'}, dimensions={0}, use_global_device_ids=true | all-gather | bytes 2560 | tf_op jit(solution)/shard_map/all_gather | solution.py:55
  96.1 0.1 convert_reduce_fusion
  96.3 7.5 %fusion.32 = (f32[512]{0:T(512)S(1)}, f32[512,1024]{1,0:T(8,128)S(1)}) fusion(bf16[512,3584]{1,0:T(8,128)(2,1)} %all-gather.5.cloned.1.call-done, bf16[3584,1024]{1,0:T(8,128)(2,1)} %param.17), kind=kOutput, calls=%fused_computation.57 | convolution fusion | flops 3758620160 | bytes 13109248 | tf_op jit(solution)/shard_map/dot_general | solution.py:70
  103.8 45.2 %all-gather.7.cloned.1.call-done = bf16[512,4608]{1,0:T(8,128)(2,1)} async-done(((bf16[16,4608]{1,0:T(8,128)(2,1)}), bf16[512,4608]{1,0:T(8,128)(2,1)}) %all-gather.7.cloned.1.call-update) | async-done | bytes 4718608 | tf_op jit(solution)/shard_map/all_gather | solution.py:61
  149.0 10.1 %fusion.31 = (f32[512]{0:T(512)S(1)}, f32[512,1024]{1,0:T(8,128)}) fusion(bf16[512,4608]{1,0:T(8,128)(2,1)} %all-gather.7.cloned.1.call-done, bf16[4608,1024]{1,0:T(8,128)(2,1)} %param.14), kind=kOutput, calls=%fused_computation.56 | convolution fusion | flops 4832361984 | bytes 16254976 | tf_op jit(solution)/shard_map/dot_general | solution.py:69
  159.1 39.0 %all-reduce.1 = (f32[512]{0:T(512)S(1)}, f32[512]{0:T(512)S(1)}) all-reduce(f32[512]{0:T(512)S(1)} %get-tuple-element.16, f32[512]{0:T(512)S(1)} %get-tuple-element.18), channel_id=1, replica_groups=mesh['dp'=4,'tp'=8] {'dp','tp'}, use_global_device_ids=true, to_apply=%region_12.13 | all-reduce | flops 1024 | bytes 8192 | tf_op jit(solution)/shard_map/pmax | solution.py:75
  198.1 2.8 multiply_reduce_fusion
  200.9 40.1 %all-reduce = (f32[512]{0:T(512)S(1)}, f32[512]{0:T(512)S(1)}, f32[512]{0:T(512)S(1)}, f32[512]{0:T(512)S(1)}) all-reduce(f32[512]{0:T(512)S(1)} %get-tuple-element.3, f32[512]{0:T(512)S(1)} %get-tuple-element.5, f32[512]{0:T(512)S(1)} %get-tuple-element.4, f32[512]{0:T(512)S(1)} %get-tuple-element.2), channel_id=1, replica_groups=mesh['dp'=4,'tp'=8] {'dp','tp'}, use_global_device_ids=true, to_apply=%region_14.15 | all-reduce | flops 2048 | bytes 16384 | tf_op jit(solution)/shard_map/psum | solution.py:78
  241.0 11.6 %fusion.6 = f32[512,3584]{1,0:T(8,128)} fusion(bf16[3584,1024]{1,0:T(8,128)(2,1)} %param.17, f32[512,1024]{1,0:T(8,128)} %get-tuple-element.17, f32[512,1024]{1,0:T(8,128)S(1)} %get-tuple-element.19, s32[1024]{0:T(1024)S(1)} %iota_add_fusion, f32[512]{0:T(512)S(1)} %get-tuple-element.8, f32[512]{0:T(512)S(1)} %get-tuple-element.12, ...), kind=kOutput, calls=%fused_computation.11 | convolution fusion | flops 3763863552 | bytes 18890752 | tf_op jit(solution)/shard_map/dot_general | solution.py:99
  252.6 0.6 dynamic_slice.3
  253.2 162.3 %reduce-scatter.5.cloned.1.call-done = f32[16,3584]{1,0:T(8,128)} async-done(((f32[512,3584]{1,0:T(8,128)}), f32[16,3584]{1,0:T(8,128)}) %reduce-scatter.5.cloned.1.call-update) | async-done | bytes 229392 | tf_op jit(solution)/shard_map/reduce_scatter | solution.py:98
  415.5 1.1 fusion.26
  416.6 1.7 fusion.25
  (28 shorter events, 0.3 us)
Async XLA Ops:
  8.0 76.0 %copy-start.3 = (f32[4608]{0:T(1024)S(1)}, f32[4608]{0:T(1024)}, u32[]{:S(2)}) copy-start(f32[4608]{0:T(1024)} %param.12) | copy-start | bytes 55300
  8.0 76.0 %copy-start.1 = (bf16[16,4608]{1,0:T(8,128)(2,1)S(1)}, bf16[16,4608]{1,0:T(8,128)(2,1)}, u32[]{:S(2)}) copy-start(bf16[16,4608]{1,0:T(8,128)(2,1)} %param.11) | copy-start | bytes 442372
  8.0 76.0 %copy-start.4 = (f32[4608]{0:T(1024)S(1)}, f32[4608]{0:T(1024)}, u32[]{:S(2)}) copy-start(f32[4608]{0:T(1024)} %param.13) | copy-start | bytes 55300
  8.0 77.8 %copy-start.5 = (s32[1,8]{1,0:T(1,128)S(1)}, s32[1,8]{1,0:T(1,128)}, u32[]{:S(2)}) copy-start(s32[1,8]{1,0:T(1,128)} %param.19) | copy-start | bytes 100
  8.0 83.0 %copy-start.6 = (s32[128]{0:T(128)S(1)}, s32[128]{0:T(128)}, u32[]{:S(2)}) copy-start(s32[128]{0:T(128)} %param.18) | copy-start | bytes 1540
  8.1 73.6 %reduce-scatter.3.cloned.1.call-start = ((), (), s32[]{:S(2)}) async-start(), calls=%async_computation.3 | async-start | bytes 1327104 | tf_op jit(solution)/shard_map/reduce_scatter | solution.py:42
  8.8 87.5 %all-gather.5.cloned.1.call-start = ((), (), s32[]{:S(2)}) async-start(), calls=%async_computation.2 | async-start | bytes 3784704 | tf_op jit(solution)/shard_map/all_gather | solution.py:62
  11.6 137.4 %all-gather.7.cloned.1.call-start = ((), (), s32[]{:S(2)}) async-start(), calls=%async_computation.4 | async-start | bytes 4866048 | tf_op jit(solution)/shard_map/all_gather | solution.py:61
  85.8 329.8 %reduce-scatter.5.cloned.1.call-start = ((), (), s32[]{:S(2)}) async-start(), calls=%async_computation.5 | async-start | bytes 7569408 | tf_op jit(solution)/shard_map/reduce_scatter | solution.py:98
  252.6 162.9 %copy-start = (bf16[16,3584]{1,0:T(8,128)(2,1)S(1)}, bf16[16,3584]{1,0:T(8,128)(2,1)}, u32[]{:S(2)}) copy-start(bf16[16,3584]{1,0:T(8,128)(2,1)} %param.15) | copy-start | bytes 344068
  252.6 162.9 %copy-start.2 = (f32[3584]{0:T(1024)S(1)}, f32[3584]{0:T(1024)}, u32[]{:S(2)}) copy-start(f32[3584]{0:T(1024)} %param.16) | copy-start | bytes 43012
Sparse Core Ops, SparseCore 0:
  12.2 69.3 reduce-scatter.2
Sparse Core Ops, SparseCore 1:
  12.1 64.3 all-gather.4
  85.9 63.1 all-gather.6
  252.7 162.8 reduce-scatter.4
where the time goes:
time: 426 us
  waiting for transfers between devices  278 us (65%)
  blocking collectives  89.2 us (21%)
  matrix products  29.2 us (7%)
  between operations  15.8 us (4%)
  other arithmetic  12.6 us (3%)
    reduce_scatter x1, waiting for transfers between devices, shards(): lax.psum_scatter(lax.dot_general(logit_grad, student_head, (((1,), (1,)),...  162 us
    reduce_scatter x1, waiting for transfers between devices, shards(): lax.psum_scatter(teacher_partial[0].astype(jnp.float32).astype(jnp.bfloat...  70.1 us
    all_gather x1, waiting for transfers between devices, shards(): lax.all_gather(teacher_norm, ('dp', 'tp'), axis=0, tiled=True)  45.2 us
    psum x1, blocking collectives, shards(): lax.psum((jnp.sum(t_exp, axis=1), jnp.sum(t_exp * (t_logits - s_logits),...  40.1 us
    pmax x1, blocking collectives, shards(): t_max, s_max = lax.pmax((t_local, s_local), ('dp', 'tp'))  39 us
    dot_general x1, matrix products, shards(): lax.dot_general(logit_grad, student_head, (((1,), (1,)), ((), ())), prefe...  11.6 us
    dot_general x1, matrix products, shards(): jnp.dot(whole_t, teacher_head, preferred_element_type=jnp.float32)  10.1 us
  transfers between devices with their start and end apart: 4, of which 3 were waited for; matrix products, arithmetic and copies ran while one was open for 4% of the time, Pallas kernels for 0%

commit v1 on v0

--- a/solution.py
+++ b/solution.py
@@ -2,6 +2,7 @@
 import jax.numpy as jnp
 from jax import lax
 from jax.sharding import PartitionSpec as P
+from jax.lax import psum
 
 EPS = 1e-06
 BETA = 0.5
@@ -37,6 +38,12 @@
     labels,
     lengths,
 ):
+
+    def zones_replace(vals):
+        for dd in ("tp", "dp"):
+            vals = psum(vals, dd)
+        return vals
+
     share = teacher_residual.shape[0]
     tok_rows = labels.shape[0]
     mlp_sum = lax.psum_scatter(
@@ -75,14 +82,13 @@
     t_max, s_max = lax.pmax((t_local, s_local), ("dp", "tp"))
     t_exp = jnp.exp(t_logits - t_max[:, None])
     s_exp = jnp.exp(s_logits - s_max[:, None])
-    t_total, t_cross, s_total, label_value = lax.psum(
+    t_total, t_cross, s_total, label_value = zones_replace(
         (
             jnp.sum(t_exp, axis=1),
             jnp.sum(t_exp * (t_logits - s_logits), axis=1),
             jnp.sum(s_exp, axis=1),
             label_logit,
-        ),
-        ("dp", "tp"),
+        )
     )
     t_log = t_max + jnp.log(t_total)
     s_log = s_max + jnp.log(s_total)

time: 426 us -> 412 us (0.967)
  blocking collectives: 89.2 us -> 75.6 us
    psum x1 -> x2, blocking collectives: 40.1 us -> 26.5 us  [zones_replace(): vals = psum(vals, dd)]
where the time goes in v1:
time: 412 us; the launch traced here: 410 us
  waiting for transfers between devices  276 us (67%)
  blocking collectives  75.6 us (18%)
  matrix products  29.2 us (7%)
  between operations  15.8 us (4%)
  other arithmetic  12.6 us (3%)
    reduce_scatter x1, waiting for transfers between devices, shards(): lax.psum_scatter(lax.dot_general(logit_grad, student_head, (((1,), (1,)),...  160 us
    reduce_scatter x1, waiting for transfers between devices, shards(): lax.psum_scatter(teacher_partial[0].astype(jnp.float32).astype(jnp.bfloat...  70.1 us
    all_gather x1, waiting for transfers between devices, shards(): lax.all_gather(teacher_norm, ('dp', 'tp'), axis=0, tiled=True)  45.2 us
    pmax x1, blocking collectives, shards(): t_max, s_max = lax.pmax((t_local, s_local), ('dp', 'tp'))  39 us
    psum x2, blocking collectives, zones_replace(): vals = psum(vals, dd)  26.5 us
    dot_general x1, matrix products, shards(): lax.dot_general(logit_grad, student_head, (((1,), (1,)), ((), ())), prefe...  11.6 us
    dot_general x1, matrix products, shards(): jnp.dot(whole_t, teacher_head, preferred_element_type=jnp.float32)  10.1 us
  transfers between devices with their start and end apart: 4, of which 3 were waited for; matrix products, arithmetic and copies ran while one was open for 4% of the time, Pallas kernels for 0%

profile of v1, /device:TPU:0, one launch (start us, length us, event | category | flops | bytes accessed | tf_op | source)
XLA Modules:
  0.0 410.5 jit_solution(9961711488785132773)
XLA Ops:
  8.1 0.7 reduce-scatter.3.cloned.1.call-update
  8.8 1.0 fusion.21
  9.9 1.7 fusion.23
  11.6 0.0 all-gather.7.cloned.1.call-start
  11.6 70.1 %reduce-scatter.3.cloned.1.call-done = bf16[16,4608]{1,0:T(8,128)(2,1)} async-done(((bf16[128,4608]{1,0:T(8,128)(2,1)}), bf16[16,4608]{1,0:T(8,128)(2,1)}) %reduce-scatter.3.cloned.1.call-update) | async-done | bytes 147472 | tf_op jit(solution)/shard_map/reduce_scatter | solution.py:49
  81.7 1.1 fusion.18
  82.8 1.2 multiply_reduce_fusion.1
  84.0 1.7 multiply_convert_fusion
  85.8 5.1 %all-gather = s32[4,1,8]{2,1,0:T(1,128)S(1)} all-gather(s32[1,1,8]{2,1,0:T(1,128)S(1)} %bitcast.20), channel_id=1, replica_groups=mesh['dp'=4,'tp'=8] {'dp'}, dimensions={0}, use_global_device_ids=true | all-gather | bytes 160 | tf_op jit(solution)/shard_map/all_gather | solution.py:63
  90.9 0.2 reduce_window_sum.11
  91.1 5.0 %all-gather.1 = s32[4,1,128]{2,1,0:T(1,128)S(1)} all-gather(s32[1,1,128]{2,1,0:T(1,128)S(1)} %bitcast.21), channel_id=1, replica_groups=mesh['dp'=4,'tp'=8] {'dp'}, dimensions={0}, use_global_device_ids=true | all-gather | bytes 2560 | tf_op jit(solution)/shard_map/all_gather | solution.py:62
  96.1 0.1 convert_reduce_fusion
  96.3 7.5 %fusion.32 = (f32[512]{0:T(512)S(1)}, f32[512,1024]{1,0:T(8,128)S(1)}) fusion(bf16[512,3584]{1,0:T(8,128)(2,1)} %all-gather.5.cloned.1.call-done, bf16[3584,1024]{1,0:T(8,128)(2,1)} %param.17), kind=kOutput, calls=%fused_computation.57 | convolution fusion | flops 3758620160 | bytes 13109248 | tf_op jit(solution)/shard_map/dot_general | solution.py:77
  103.8 45.2 %all-gather.7.cloned.1.call-done = bf16[512,4608]{1,0:T(8,128)(2,1)} async-done(((bf16[16,4608]{1,0:T(8,128)(2,1)}), bf16[512,4608]{1,0:T(8,128)(2,1)}) %all-gather.7.cloned.1.call-update) | async-done | bytes 4718608 | tf_op jit(solution)/shard_map/all_gather | solution.py:68
  149.0 10.1 %fusion.31 = (f32[512]{0:T(512)S(1)}, f32[512,1024]{1,0:T(8,128)}) fusion(bf16[512,4608]{1,0:T(8,128)(2,1)} %all-gather.7.cloned.1.call-done, bf16[4608,1024]{1,0:T(8,128)(2,1)} %param.14), kind=kOutput, calls=%fused_computation.56 | convolution fusion | flops 4832361984 | bytes 16254976 | tf_op jit(solution)/shard_map/dot_general | solution.py:76
  159.1 39.0 %all-reduce = (f32[512]{0:T(512)S(1)}, f32[512]{0:T(512)S(1)}) all-reduce(f32[512]{0:T(512)S(1)} %get-tuple-element.20, f32[512]{0:T(512)S(1)} %get-tuple-element.22), channel_id=1, replica_groups=mesh['dp'=4,'tp'=8] {'dp','tp'}, use_global_device_ids=true, to_apply=%region_13.14 | all-reduce | flops 1024 | bytes 8192 | tf_op jit(solution)/shard_map/pmax | solution.py:82
  198.1 2.8 multiply_reduce_fusion
  200.9 20.8 %all-reduce.1 = (f32[512]{0:T(512)S(1)}, f32[512]{0:T(512)S(1)}, f32[512]{0:T(512)S(1)}, f32[512]{0:T(512)S(1)}) all-reduce(f32[512]{0:T(512)S(1)} %get-tuple-element.3, f32[512]{0:T(512)S(1)} %get-tuple-element.5, f32[512]{0:T(512)S(1)} %get-tuple-element.4, f32[512]{0:T(512)S(1)} %get-tuple-element.2), channel_id=1, replica_groups=mesh['dp'=4,'tp'=8] {'tp'}, use_global_device_ids=true, to_apply=%region_15.16 | all-reduce | flops 2048 | bytes 16384 | tf_op jit(solution)/shard_map/psum | solution.py:44
  221.7 5.7 %all-reduce.2 = (f32[512]{0:T(512)S(1)}, f32[512]{0:T(512)S(1)}, f32[512]{0:T(512)S(1)}, f32[512]{0:T(512)S(1)}) all-reduce(f32[512]{0:T(512)S(1)} %get-tuple-element.10, f32[512]{0:T(512)S(1)} %get-tuple-element.11, f32[512]{0:T(512)S(1)} %get-tuple-element.12, f32[512]{0:T(512)S(1)} %get-tuple-element.13), channel_id=1, replica_groups=mesh['dp'=4,'tp'=8] {'dp'}, use_global_device_ids=true, to_apply=%region_16.17 | all-reduce | flops 2048 | bytes 16384 | tf_op jit(solution)/shard_map/psum | solution.py:44
  227.4 11.6 %fusion.6 = f32[512,3584]{1,0:T(8,128)} fusion(bf16[3584,1024]{1,0:T(8,128)(2,1)} %param.17, f32[512,1024]{1,0:T(8,128)} %get-tuple-element.21, f32[512,1024]{1,0:T(8,128)S(1)} %get-tuple-element.23, s32[1024]{0:T(1024)S(1)} %iota_add_fusion, f32[512]{0:T(512)S(1)} %get-tuple-element.14, f32[512]{0:T(512)S(1)} %get-tuple-element.8, ...), kind=kOutput, calls=%fused_computation.11 | convolution fusion | flops 3763863552 | bytes 18890752 | tf_op jit(solution)/shard_map/dot_general | solution.py:105
  239.1 0.6 dynamic_slice.3
  239.7 160.4 %reduce-scatter.5.cloned.1.call-done = f32[16,3584]{1,0:T(8,128)} async-done(((f32[512,3584]{1,0:T(8,128)}), f32[16,3584]{1,0:T(8,128)}) %reduce-scatter.5.cloned.1.call-update) | async-done | bytes 229392 | tf_op jit(solution)/shard_map/reduce_scatter | solution.py:104
  400.0 1.1 fusion.26
  401.1 1.7 fusion.25
  (29 shorter events, 0.3 us)
Async XLA Ops:
  8.0 76.0 %copy-start.3 = (f32[4608]{0:T(1024)S(1)}, f32[4608]{0:T(1024)}, u32[]{:S(2)}) copy-start(f32[4608]{0:T(1024)} %param.12) | copy-start | bytes 55300
  8.0 76.0 %copy-start.1 = (bf16[16,4608]{1,0:T(8,128)(2,1)S(1)}, bf16[16,4608]{1,0:T(8,128)(2,1)}, u32[]{:S(2)}) copy-start(bf16[16,4608]{1,0:T(8,128)(2,1)} %param.11) | copy-start | bytes 442372
  8.0 76.0 %copy-start.4 = (f32[4608]{0:T(1024)S(1)}, f32[4608]{0:T(1024)}, u32[]{:S(2)}) copy-start(f32[4608]{0:T(1024)} %param.13) | copy-start | bytes 55300
  8.0 77.8 %copy-start.5 = (s32[1,8]{1,0:T(1,128)S(1)}, s32[1,8]{1,0:T(1,128)}, u32[]{:S(2)}) copy-start(s32[1,8]{1,0:T(1,128)} %param.19) | copy-start | bytes 100
  8.0 83.0 %copy-start.6 = (s32[128]{0:T(128)S(1)}, s32[128]{0:T(128)}, u32[]{:S(2)}) copy-start(s32[128]{0:T(128)} %param.18) | copy-start | bytes 1540
  8.1 73.6 %reduce-scatter.3.cloned.1.call-start = ((), (), s32[]{:S(2)}) async-start(), calls=%async_computation.3 | async-start | bytes 1327104 | tf_op jit(solution)/shard_map/reduce_scatter | solution.py:49
  8.8 87.5 %all-gather.5.cloned.1.call-start = ((), (), s32[]{:S(2)}) async-start(), calls=%async_computation.2 | async-start | bytes 3784704 | tf_op jit(solution)/shard_map/all_gather | solution.py:69
  11.6 137.4 %all-gather.7.cloned.1.call-start = ((), (), s32[]{:S(2)}) async-start(), calls=%async_computation.4 | async-start | bytes 4866048 | tf_op jit(solution)/shard_map/all_gather | solution.py:68
  85.8 314.3 %reduce-scatter.5.cloned.1.call-start = ((), (), s32[]{:S(2)}) async-start(), calls=%async_computation.5 | async-start | bytes 7569408 | tf_op jit(solution)/shard_map/reduce_scatter | solution.py:104
  239.0 161.0 %copy-start = (bf16[16,3584]{1,0:T(8,128)(2,1)S(1)}, bf16[16,3584]{1,0:T(8,128)(2,1)}, u32[]{:S(2)}) copy-start(bf16[16,3584]{1,0:T(8,128)(2,1)} %param.15) | copy-start | bytes 344068
  239.0 161.0 %copy-start.2 = (f32[3584]{0:T(1024)S(1)}, f32[3584]{0:T(1024)}, u32[]{:S(2)}) copy-start(f32[3584]{0:T(1024)} %param.16) | copy-start | bytes 43012
Sparse Core Ops, SparseCore 0:
  12.2 69.3 reduce-scatter.2
Sparse Core Ops, SparseCore 1:
  12.1 64.3 all-gather.4
  85.9 63.1 all-gather.6
  239.1 160.8 reduce-scatter.4
